TPU v7x, 256 devices: a whole 4x4x8 slice. The times are simulated.
256 devices in a mesh: tensor: 64 (over z_lo, x, y, core), dp: 4 (over z_hi).
Axes of the slice: x: 4, y: 4, z: 8 (z_hi: 4, z_lo: 2; z = z_hi * 2 + z_lo), core: 2. Of those that a mesh axis runs over, the one named last changes fastest.
Arguments:
- cotangent: bfloat16 [1024, 8192], P('dp', 'tensor'), may hold values from -12 to 12
- down_weight: bfloat16 [28672, 8192], P('tensor', 'dp'), may hold values from -0.0625 to 0.0625
- gate_pre: bfloat16 [1024, 28672], P('dp', 'tensor'), may hold values from -6 to 6
- up_pre: bfloat16 [1024, 28672], P('dp', 'tensor'), may hold values from -6 to 6
Outputs:
- factor: bfloat16 [64, 2, 33, 4, 50176], P('tensor', None, None, 'dp')
All inputs are finite; a program needn't handle non-finite values.
Results may differ from a plain program's by a relative error of at most 0.0057.
Values may be sent and summed in bfloat16 or wider, within the bound.
A program may use at most 128 MiB of HBM per device.

v0:
```python
import jax
import jax.numpy as jnp
from jax import lax
from jax.sharding import PartitionSpec as P


def per_device(cotangent, down_weight, gate_pre, up_pre):
    block_count = lax.axis_size("tensor")
    groups = lax.axis_size("dp")
    own_block = lax.axis_index("tensor")
    group_index = lax.axis_index("dp")
    local_tokens = gate_pre.shape[0]
    block_width = gate_pre.shape[1]
    slice_width = block_width // groups
    all_tokens = local_tokens * groups
    band_width = block_count // 2 + 1
    contract = (((1,), (1,)), ((), ()))
    features = lax.all_gather(cotangent, "tensor", axis=1, tiled=True)
    hidden_cot = lax.dot_general(
        features,
        lax.all_gather(down_weight, "dp", axis=1, tiled=True),
        contract,
        preferred_element_type=jnp.float32,
    )
    gate_value = gate_pre.astype(jnp.float32)
    up_value = up_pre.astype(jnp.float32)
    sigmoid_gate = jax.nn.sigmoid(gate_value)
    grad_gate = (
        hidden_cot * up_value * sigmoid_gate * (1.0 + gate_value * (1.0 - sigmoid_gate))
    ).astype(jnp.bfloat16)
    grad_up = (hidden_cot * gate_value * sigmoid_gate).astype(jnp.bfloat16)
    stacked = jnp.stack([grad_gate, grad_up])
    own_rows = lax.all_gather(stacked, "dp", axis=1, tiled=True)
    own_slice = lax.dynamic_slice_in_dim(own_rows, group_index * slice_width, slice_width, 2)
    inverse_count = 1.0 / all_tokens

    def factor_tile(partner):
        product = jnp.einsum("ftr,ftc->frc", own_rows, partner, preferred_element_type=jnp.float32)
        return (product * inverse_count).astype(jnp.bfloat16)

    def place(result, offset, partner):
        return lax.dynamic_update_slice(
            result,
            factor_tile(partner)[:, None],
            (jnp.int32(0), offset, jnp.int32(0), jnp.int32(0)),
        )

    holder = jnp.zeros((2, band_width, block_width, slice_width), jnp.bfloat16)
    block_piece = lax.all_gather(own_slice[None], "tensor", axis=0, tiled=True)

    def place_block(position, current):
        offset = (own_block - position) % block_count
        partner = lax.dynamic_index_in_dim(block_piece, position, 0, keepdims=False)
        return lax.cond(
            offset < band_width,
            lambda kept: place(kept, offset, partner),
            lambda kept: kept,
            current,
        )

    factor = lax.fori_loop(0, block_piece.shape[0], place_block, holder)
    flat = factor.reshape(2, band_width, block_width * slice_width)
    return flat[None, :, :, None, :]


def solution(mesh):
    placed = (P("dp", "tensor"), P("tensor", "dp"), P("dp", "tensor"), P("dp", "tensor"))
    return jax.shard_map(
        per_device,
        mesh=mesh,
        in_specs=placed,
        out_specs=P("tensor", None, None, "dp", None),
        check_vma=False,
    )
```

profile of v0, /device:TPU:1, one launch (start us, length us, event | category | flops | bytes accessed | tf_op | source)
XLA Modules:
  0.0 617.8 jit_solution(3863569441559747056)
XLA Ops:
  8.1 121.4 %all-gather.6.cloned.1.call-done = bf16[256,8192]{1,0:T(8,128)(2,1)} async-done(((bf16[256,128]{1,0:T(8,128)(2,1)}), bf16[256,8192]{1,0:T(8,128)(2,1)}) %all-gather.6.cloned.1.call-update) | async-done | bytes 4194320 | tf_op jit(solution)/shard_map/all_gather | solution.py:18
  129.5 137.8 %all-gather.8.cloned.1.call-done = bf16[448,8192]{1,0:T(8,128)(2,1)} async-done(((bf16[448,2048]{1,0:T(8,128)(2,1)}), bf16[448,8192]{1,0:T(8,128)(2,1)}) %all-gather.8.cloned.1.call-update) | async-done | bytes 7340048 | tf_op jit(solution)/shard_map/all_gather | solution.py:21
  267.3 6.5 %fusion.15 = (bf16[1,256,448]{1,2,0:T(8,128)(2,1)S(1)}, bf16[1,256,448]{1,2,0:T(8,128)(2,1)S(1)}) fusion(bf16[256,448]{0,1:T(8,128)(2,1)} %param.10, bf16[256,448]{0,1:T(8,128)(2,1)} %param.11, bf16[256,8192]{1,0:T(8,128)(2,1)} %all-gather.6.cloned.1.call-done, bf16[448,8192]{1,0:T(8,128)(2,1)} %all-gather.8.cloned.1.call-done), kind=kOutput, calls=%fused_computation.20 | convolution fusion | flops 1880768512 | bytes 12451840 | tf_op jit(solution)/shard_map/dot_general | solution.py:19
  274.7 50.5 %all-gather.10.cloned.1.call-done = bf16[2,1024,448]{1,2,0:T(8,128)(2,1)} async-done(((bf16[2,256,448]{1,2,0:T(8,128)(2,1)}), bf16[2,1024,448]{1,2,0:T(8,128)(2,1)}) %all-gather.10.cloned.1.call-update) | async-done | bytes 1835024 | tf_op jit(solution)/shard_map/all_gather | solution.py:33
  327.2 167.3 %all-gather.12.cloned.1.call-done = bf16[128,1024,112]{1,2,0:T(8,128)(2,1)} async-done(((bf16[2,1024,112]{1,2,0:T(8,128)(2,1)}), bf16[128,1024,112]{1,2,0:T(8,128)(2,1)}) %all-gather.12.cloned.1.call-update) | async-done | bytes 29360144 | tf_op jit(solution)/shard_map/all_gather | solution.py:49
  494.4 3.9 broadcast_in_dim.10
  498.4 80.2 %while.18 = (s32[]{:T(128)}, bf16[2,33,448,112]{2,3,0,1:T(8,128)(2,1)}, s32[]{:T(128)}, bf16[64,2,1024,112]{2,3,1,0:T(8,128)(2,1)}, bf16[2,1024,448]{1,2,0:T(8,1...) while((s32[]{:T(128)}, bf16[2,33,448,112]{2,3,0,1:T(8,128)(2,1)}, s32[]{:T(128)}, ...), condition=%wide.region_3.4_spmd, body=%wide.region_0.3_spmd.sunk | while | flops 205721616 | bytes 2523496 | solution.py:61
  498.4 2.4 conditional.2
  498.4 2.4 fusion.2
  500.8 2.4 conditional.2
  500.8 2.4 fusion.2
  504.5 2.4 conditional.2
  504.6 2.4 fusion.2
  514.1 2.4 conditional.2
  514.1 2.4 fusion.2
  516.5 2.4 conditional.2
  516.5 2.4 fusion.2
  521.3 2.4 conditional.2
  521.3 2.4 fusion.2
  526.1 2.4 conditional.2
  526.1 2.4 fusion.2
  528.5 2.4 conditional.2
  528.5 2.4 fusion.2
  530.9 2.4 conditional.2
  533.2 2.4 conditional.2
  533.2 2.4 fusion.2
  542.8 2.4 conditional.2
  542.8 2.4 fusion.2
  552.3 2.4 conditional.2
  552.3 2.4 fusion.2
  554.7 2.4 conditional.2
  554.7 2.4 fusion.2
  557.1 2.4 conditional.2
  557.1 2.4 fusion.2
  559.5 2.4 conditional.2
  559.5 2.4 fusion.2
  561.9 2.4 conditional.2
  561.9 2.4 fusion.2
  564.3 2.4 conditional.2
  564.3 2.4 fusion.2
  566.7 2.4 conditional.2
  566.7 2.4 fusion.2
  573.8 2.4 conditional.2
  573.8 2.4 fusion.2
  576.2 2.4 conditional.2
  576.2 2.4 fusion.2
  578.6 10.8 %copy.6 = bf16[2,33,448,112]{3,2,0,1:T(8,128)(2,1)} copy(bf16[2,33,448,112]{2,3,0,1:T(8,128)(2,1)} %get-tuple-element.191) | data formatting | bytes 13246464 | tf_op jit(solution)/shard_map/while | solution.py:61
  589.5 21.8 %broadcast_in_dim_reshape.3 = bf16[1,2,33,1,50176]{4,1,3,2,0:T(2,128)(2,1)} reshape(bf16[2,33,448,112]{3,2,0,1:T(8,128)(2,1)} %copy.6) | data formatting | bytes 13246464 | tf_op jit(solution)/shard_map/broadcast_in_dim;reshape | solution.py:63
  (70 shorter events, 68.9 us)
Async XLA Ops:
  6.5 122.9 %all-gather.6.cloned.1.call-start = ((), (), s32[]{:S(2)}) async-start(), calls=%async_computation | async-start | bytes 4259840 | tf_op jit(solution)/shard_map/all_gather | solution.py:18
  7.3 260.0 %all-gather.8.cloned.1.call-start = ((), (), s32[]{:S(2)}) async-start(), calls=%async_computation.1 | async-start | bytes 9175040 | tf_op jit(solution)/shard_map/all_gather | solution.py:21
  8.0 317.2 %all-gather.10.cloned.1.call-start = ((), (), s32[]{:S(2)}) async-start(), calls=%async_computation.2 | async-start | bytes 2293760 | tf_op jit(solution)/shard_map/all_gather | solution.py:33
  274.7 219.8 %all-gather.12.cloned.1.call-start = ((), (), s32[]{:S(2)}) async-start(), calls=%async_computation.3 | async-start | bytes 29818880 | tf_op jit(solution)/shard_map/all_gather | solution.py:49
  325.2 173.2 %copy-start = (bf16[2,1024,448]{1,2,0:T(8,128)(2,1)S(1)}, bf16[2,1024,448]{1,2,0:T(8,128)(2,1)}, u32[]{:S(2)}) copy-start(bf16[2,1024,448]{1,2,0:T(8,128)(2,1)} %all-gather.10.cloned.1.call-done) | copy-start | bytes 5505028
Sparse Core Ops, SparseCore 0:
  9.1 120.3 all-gather.5
  131.3 135.9 all-gather.7
  274.8 50.3 all-gather.9
  327.3 167.1 all-gather.11
where the time goes:
time: 620 us; the launch traced here: 618 us
  waiting for transfers between devices  478 us (77%)
  matrix products  85.4 us (14%)
  local copies, waits for them, and re-layouts  38.5 us (6%)
  between operations  13.1 us (2%)
    all_gather x1, waiting for transfers between devices, per_device(): block_piece = lax.all_gather(own_slice[None], 'tensor', axis=0, tiled=True)  167 us
    all_gather x1, waiting for transfers between devices, per_device(): lax.all_gather(down_weight, 'dp', axis=1, tiled=True)  138 us
    all_gather x1, waiting for transfers between devices, per_device(): features = lax.all_gather(cotangent, 'tensor', axis=1, tiled=True)  121 us
    dot_general x33, matrix products, factor_tile(): jnp.einsum('ftr,ftc->frc', own_rows, partner, preferred_element_type=jnp....  78.8 us
    all_gather x1, waiting for transfers between devices, per_device(): own_rows = lax.all_gather(stacked, 'dp', axis=1, tiled=True)  50.5 us
    another operation x1, local copies, waits for them, and re-layouts, per_device(): return flat[None, :, :, None, :]  21.8 us
  transfers between devices with their start and end apart: 4, of which 4 were waited for; matrix products, arithmetic and copies ran while one was open for 0% of the time, Pallas kernels for 0%

commit v1 on v0

--- a/solution.py
+++ b/solution.py
@@ -46,7 +46,10 @@
         )
 
     holder = jnp.zeros((2, band_width, block_width, slice_width), jnp.bfloat16)
-    block_piece = lax.all_gather(own_slice[None], "tensor", axis=0, tiled=True)
+    block_piece = jnp.concatenate(
+        lax.all_to_all(jnp.stack([own_slice[None]] * lax.axis_size("tensor")), "tensor", 0, 0),
+        axis=0,
+    )
 
     def place_block(position, current):
         offset = (own_block - position) % block_count

time: 620 us -> 906 us (1.46); the launches traced: 618 us -> 893 us
  waiting for transfers between devices: 478 us -> 738 us
    all_to_all x0 -> x1, waiting for transfers between devices: none -> 427 us  [per_device(): lax.all_to_all(jnp.stack([own_slice[None]] * lax.axis_size('tensor')), 't...]
    all_gather x1 -> x0, waiting for transfers between devices: 167 us -> none  [per_device(): block_piece = lax.all_gather(own_slice[None], 'tensor', axis=0, tiled=True)]
    another operation x0 -> x1, local copies, waits for them, and re-layouts: none -> 9.88 us  [per_device(): jnp.stack([own_slice[None]] * lax.axis_size('tensor'))]
where the time goes in v1:
time: 906 us; the launch traced here: 893 us
  waiting for transfers between devices  738 us (81%)
  matrix products  85.2 us (9%)
  local copies, waits for them, and re-layouts  47.5 us (5%)
  between operations  13.1 us (1%)
    all_to_all x1, waiting for transfers between devices, per_device(): lax.all_to_all(jnp.stack([own_slice[None]] * lax.axis_size('tensor')), 't...  427 us
    all_gather x1, waiting for transfers between devices, per_device(): lax.all_gather(down_weight, 'dp', axis=1, tiled=True)  138 us
    all_gather x1, waiting for transfers between devices, per_device(): features = lax.all_gather(cotangent, 'tensor', axis=1, tiled=True)  121 us
    dot_general x33, matrix products, factor_tile(): jnp.einsum('ftr,ftc->frc', own_rows, partner, preferred_element_type=jnp....  78.7 us
    all_gather x1, waiting for transfers between devices, per_device(): own_rows = lax.all_gather(stacked, 'dp', axis=1, tiled=True)  50.5 us
    another operation x1, local copies, waits for them, and re-layouts, per_device(): return flat[None, :, :, None, :]  21.8 us
  transfers between devices with their start and end apart: 4, of which 4 were waited for; matrix products, arithmetic and copies ran while one was open for 0% of the time, Pallas kernels for 0%

profile of v1, /device:TPU:1, one launch (start us, length us, event | category | flops | bytes accessed | tf_op | source)
XLA Modules:
  0.0 893.3 jit_solution(12596353697504210007)
XLA Ops:
  8.1 121.4 %all-gather.4.cloned.1.call-done = bf16[256,8192]{1,0:T(8,128)(2,1)} async-done(((bf16[256,128]{1,0:T(8,128)(2,1)}), bf16[256,8192]{1,0:T(8,128)(2,1)}) %all-gather.4.cloned.1.call-update) | async-done | bytes 4194320 | tf_op jit(solution)/shard_map/all_gather | solution.py:18
  129.5 137.8 %all-gather.6.cloned.1.call-done = bf16[448,8192]{1,0:T(8,128)(2,1)} async-done(((bf16[448,2048]{1,0:T(8,128)(2,1)}), bf16[448,8192]{1,0:T(8,128)(2,1)}) %all-gather.6.cloned.1.call-update) | async-done | bytes 7340048 | tf_op jit(solution)/shard_map/all_gather | solution.py:21
  267.3 6.5 fusion.15
  274.6 50.5 %all-gather.8.cloned.1.call-done = bf16[2,1024,448]{1,2,0:T(8,128)(2,1)} async-done(((bf16[2,256,448]{1,2,0:T(8,128)(2,1)}), bf16[2,1024,448]{1,2,0:T(8,128)(2,1)}) %all-gather.8.cloned.1.call-update) | async-done | bytes 1835024 | tf_op jit(solution)/shard_map/all_gather | solution.py:33
  326.2 9.9 %stack.15 = bf16[64,1,2,1024,112]{3,4,2,1,0:T(8,128)(2,1)} broadcast(bf16[2,1024,112]{1,2,0:T(8,128)(2,1)S(1)} %constant_dynamic-slice_fusion), dimensions={2,3,4} | broadcast | bytes 29818880 | tf_op jit(solution)/shard_map/stack | solution.py:50
  336.1 7.1 all-to-all-start
  343.2 426.9 %all-to-all-done = bf16[64,1,2,1024,112]{3,4,2,1,0:T(8,128)(2,1)} async-done(((bf16[64,1,2,1024,112]{3,4,2,1,0:T(8,128)(2,1)}), bf16[64,1,2,1024,112]{3,4,2,1,0:T(8,128)(2,1)}, u32[]{:S(2)}, u32[]{:S(2)}) %all-to-all-start) | async-done | bytes 29360160 | tf_op jit(solution)/shard_map/all_to_all | solution.py:50
  770.1 3.9 broadcast_in_dim.7
  774.0 80.1 %while.18 = (s32[]{:T(128)}, bf16[2,33,448,112]{2,3,0,1:T(8,128)(2,1)}, s32[]{:T(128)}, bf16[64,2,1024,112]{2,3,1,0:T(8,128)(2,1)}, bf16[2,1024,448]{1,2,0:T(8,1...) while((s32[]{:T(128)}, bf16[2,33,448,112]{2,3,0,1:T(8,128)(2,1)}, s32[]{:T(128)}, ...), condition=%wide.region_3.4_spmd, body=%wide.region_0.3_spmd.sunk | while | flops 205721616 | bytes 2523496 | solution.py:64
  774.0 2.4 conditional.2
  774.0 2.4 fusion.2
  776.5 2.4 conditional.2
  776.5 2.4 fusion.2
  780.2 2.4 conditional.2
  780.2 2.4 fusion.2
  785.0 2.4 conditional.2
  785.0 2.4 fusion.2
  787.4 2.4 conditional.2
  787.4 2.4 fusion.2
  789.8 2.4 conditional.2
  789.8 2.4 fusion.2
  792.1 2.4 conditional.2
  792.1 2.4 fusion.2
  801.7 2.4 conditional.2
  801.7 2.4 fusion.2
  808.8 2.4 conditional.2
  808.8 2.4 fusion.2
  813.6 2.4 conditional.2
  816.0 2.4 conditional.2
  820.7 2.4 conditional.2
  823.1 2.4 conditional.2
  823.1 2.4 fusion.2
  827.9 2.4 conditional.2
  827.9 2.4 fusion.2
  830.3 2.4 conditional.2
  832.7 2.4 conditional.2
  832.7 2.4 fusion.2
  835.1 2.4 conditional.2
  837.5 2.4 conditional.2
  837.5 2.4 fusion.2
  839.8 2.4 conditional.2
  839.9 2.4 fusion.2
  849.4 2.4 conditional.2
  849.4 2.4 fusion.2
  851.8 2.4 conditional.2
  851.8 2.4 fusion.2
  854.2 10.8 %copy.6 = bf16[2,33,448,112]{3,2,0,1:T(8,128)(2,1)} copy(bf16[2,33,448,112]{2,3,0,1:T(8,128)(2,1)} %get-tuple-element.191) | data formatting | bytes 13246464 | tf_op jit(solution)/shard_map/while | solution.py:64
  865.0 21.8 %broadcast_in_dim_reshape.3 = bf16[1,2,33,1,50176]{4,1,3,2,0:T(2,128)(2,1)} reshape(bf16[2,33,448,112]{3,2,0,1:T(8,128)(2,1)} %copy.6) | data formatting | bytes 13246464 | tf_op jit(solution)/shard_map/broadcast_in_dim;reshape | solution.py:66
  (70 shorter events, 72.6 us)
Async XLA Ops:
  6.5 122.9 %all-gather.4.cloned.1.call-start = ((), (), s32[]{:S(2)}) async-start(), calls=%async_computation.1 | async-start | bytes 4259840 | tf_op jit(solution)/shard_map/all_gather | solution.py:18
  7.3 260.0 %all-gather.6.cloned.1.call-start = ((), (), s32[]{:S(2)}) async-start(), calls=%async_computation.2 | async-start | bytes 9175040 | tf_op jit(solution)/shard_map/all_gather | solution.py:21
  8.0 317.1 %all-gather.8.cloned.1.call-start = ((), (), s32[]{:S(2)}) async-start(), calls=%async_computation.3 | async-start | bytes 2293760 | tf_op jit(solution)/shard_map/all_gather | solution.py:33
  336.1 434.0 %all-to-all-start = ((bf16[64,1,2,1024,112]{3,4,2,1,0:T(8,128)(2,1)}), bf16[64,1,2,1024,112]{3,4,2,1,0:T(8,128)(2,1)}, u32[]{:S(2)}, u32[]{:S(2)}) async-start(bf16[64,1,2,1024,112]{3,4,2,1,0:T(8,128)(2,1)} %stack.15), calls=%async_computation | async-start | bytes 58720256 | tf_op jit(solution)/shard_map/all_to_all | solution.py:50
  343.2 430.8 %copy-start = (bf16[2,1024,448]{1,2,0:T(8,128)(2,1)S(1)}, bf16[2,1024,448]{1,2,0:T(8,128)(2,1)}, u32[]{:S(2)}) copy-start(bf16[2,1024,448]{1,2,0:T(8,128)(2,1)} %all-gather.8.cloned.1.call-done) | copy-start | bytes 5505028
Sparse Core Ops, SparseCore 0:
  9.1 120.3 all-gather.3
  131.3 135.9 all-gather.5
  274.7 50.3 all-gather.7
